TPU v7x, 32 devices: a whole 2x2x4 slice. The times are simulated.
32 devices in a mesh: pts: 8 (over y, x, core), out: 4 (over z).
Axes of the slice: x: 2, y: 2, z: 4, core: 2. Of those that a mesh axis runs over, the one named last changes fastest.
Arguments:
- points: bfloat16 [32768, 1024], P('pts'), may hold values from -6 to 6
- coefficients: float32 [32768, 1024], P('pts', 'out'), may hold values from -4 to 4
- residual: float32 [32768, 1024], P('pts', 'out'), may hold values from -6 to 6
- blocks: int32 [3, 512], replicated, may hold values from 0 to 32767, as said below
Outputs:
- coefficients_out: float32 [32768, 1024], P('pts', 'out')
- residual_out: float32 [32768, 1024], P('pts', 'out')
Inputs may be any that keep to these rules, and one draw needn't show every extreme that they name: `blocks`: the 512 indices of a step are distinct.
All inputs are finite; a program needn't handle non-finite values.
Results may differ from a plain program's by a relative error of at most 0.0003.
Values may be sent and summed in bfloat16 or wider, within the bound.
No kernel may reach another device: no remote copies, remote signals or barrier semaphores. Data moves between devices by JAX's collectives and lax.ppermute only.
A program may use at most 128 MiB of HBM per device.

v0:
```python
import jax
import jax.numpy as jnp
from jax import lax
from jax.sharding import PartitionSpec as P

RIDGE = 0.5


def kernel(left_rows, right_rows, inverse_width):
    left_sq = jnp.sum(jnp.square(left_rows.astype(jnp.float32)), axis=1)
    right_sq = jnp.sum(jnp.square(right_rows.astype(jnp.float32)), axis=1)
    inner = lax.dot_general(
        left_rows, right_rows, (((1,), (1,)), ((), ())), preferred_element_type=jnp.float32
    )
    return jnp.exp(-inverse_width * (left_sq[:, None] + right_sq[None, :] - 2.0 * inner))


def local(points, coefficients, residual, blocks):
    local_count = points.shape[0]
    inverse_width = 1.0 / points.shape[1]
    position = lax.axis_index("pts")
    for number in range(blocks.shape[0]):
        chosen = blocks[number]
        offsets = chosen - position * local_count
        is_owned = (offsets >= 0) & (offsets < local_count)
        clipped = jnp.clip(offsets, 0, local_count - 1)
        owned_rows = jnp.where(is_owned[:, None], points[clipped].astype(jnp.float32), 0.0)
        owned_res = jnp.where(is_owned[:, None], residual[clipped], 0.0)
        summed = lax.psum(owned_rows.astype(jnp.bfloat16), "pts")
        block_res = lax.psum(owned_res, "pts")
        kernel_rows = kernel(points, summed, inverse_width)
        block_kernel = kernel(summed, summed, inverse_width)
        block_size = chosen.shape[0]
        factor = jnp.linalg.cholesky(block_kernel + RIDGE * jnp.eye(block_size, dtype=jnp.float32))
        update = jax.scipy.linalg.cho_solve((factor, True), block_res)
        product = jnp.dot(kernel_rows, update, precision=lax.Precision.HIGHEST)
        own_update = jnp.where(is_owned[:, None], update, 0.0)
        coefficients = coefficients.at[clipped].add(own_update)
        placed = jnp.zeros_like(residual).at[clipped].add(own_update)
        residual = residual - product - RIDGE * placed
    return (coefficients, residual)


def solution(mesh):
    return jax.shard_map(
        local,
        mesh=mesh,
        in_specs=(P("pts", None), P("pts", "out"), P("pts", "out"), P()),
        out_specs=(P("pts", "out"), P("pts", "out")),
        check_vma=False,
    )
```

profile of v0, /device:TPU:0, one launch (start us, length us, event | category | flops | bytes accessed | tf_op | source)
XLA Modules:
  0.0 701.5 jit_solution(9983994958240367674)
XLA Ops:
  46.6 62.1 %all-reduce.13.cloned.1.call-done = (bf16[512,1024]{1,0:T(8,128)(2,1)}, bf16[512,1024]{1,0:T(8,128)(2,1)}, bf16[512,1024]{1,0:T(8,128)(2,1)}) async-done(((bf16[512,1024]{1,0:T(8,128)(2,1)}, bf16[512,1024]{1,0:T(8,128)(2,1)}, bf16[512,1024]{1,0:T(8,128)(2,1)}), (bf16[512,1024]{1,0:T(8,128)(2,1)}, bf16[512,1024]{1,0:T(8,128)(2,1)}, bf16[512,1024]{1,0:T(8,128)(2,1)})) %all-reduce.13.cloned.1.call-update) | async-done | bytes 3145744 | tf_op jit(solution)/shard_map/psum | solution.py:29
  113.3 11.7 %cholesky.518 = f32[128,128]{1,0:T(8,128)S(1)} custom-call(f32[128,128]{1,0:T(8,128)S(1)} %cholesky.612), custom_call_target="Cholesky" | custom-call | tf_op jit(solution)/shard_map/jit(cholesky)/cholesky | solution.py:34
  125.0 9.8 %custom-call.41 = f32[1,128,128]{1,2,0:T(8,128)S(1)} custom-call(f32[1,128,128]{2,1,0:T(8,128)S(1)} %get-tuple-element.72), custom_call_target="InvertDiagBlocksLowerTriangular" | custom-call | tf_op jit(solution)/shard_map/jit(cholesky)/cholesky | solution.py:34
  135.7 12.1 %cholesky.537 = f32[128,128]{1,0:T(8,128)S(1)} custom-call(f32[128,128]{1,0:T(8,128)S(1)} %cholesky.616), custom_call_target="Cholesky" | custom-call | tf_op jit(solution)/shard_map/jit(cholesky)/cholesky | solution.py:34
  149.2 9.8 %custom-call.42 = f32[1,128,128]{1,2,0:T(8,128)S(1)} custom-call(f32[1,128,128]{2,1,0:T(8,128)S(1)} %get-tuple-element.69), custom_call_target="InvertDiagBlocksLowerTriangular" | custom-call | tf_op jit(solution)/shard_map/jit(cholesky)/cholesky | solution.py:34
  159.7 11.7 %cholesky.558 = f32[128,128]{1,0:T(8,128)S(1)} custom-call(f32[128,128]{1,0:T(8,128)S(1)} %cholesky.621), custom_call_target="Cholesky" | custom-call | tf_op jit(solution)/shard_map/jit(cholesky)/cholesky | solution.py:34
  172.0 9.8 %custom-call.43 = f32[1,128,128]{1,2,0:T(8,128)S(1)} custom-call(f32[1,128,128]{2,1,0:T(8,128)S(1)} %get-tuple-element.66), custom_call_target="InvertDiagBlocksLowerTriangular" | custom-call | tf_op jit(solution)/shard_map/jit(cholesky)/cholesky | solution.py:34
  182.4 11.9 %cholesky.575 = f32[128,128]{1,0:T(8,128)S(1)} custom-call(f32[128,128]{1,0:T(8,128)S(1)} %convolution_subtract_fusion.24), custom_call_target="Cholesky" | custom-call | tf_op jit(solution)/shard_map/jit(cholesky)/cholesky | solution.py:34
  212.4 11.7 %cholesky.446 = f32[128,128]{1,0:T(8,128)S(1)} custom-call(f32[128,128]{1,0:T(8,128)S(1)} %cholesky.599), custom_call_target="Cholesky" | custom-call | tf_op jit(solution)/shard_map/jit(cholesky)/cholesky | solution.py:34
  224.2 9.8 %custom-call.37 = f32[1,128,128]{1,2,0:T(8,128)S(1)} custom-call(f32[1,128,128]{2,1,0:T(8,128)S(1)} %get-tuple-element.82), custom_call_target="InvertDiagBlocksLowerTriangular" | custom-call | tf_op jit(solution)/shard_map/jit(cholesky)/cholesky | solution.py:34
  236.6 11.7 %cholesky.465 = f32[128,128]{1,0:T(8,128)S(1)} custom-call(f32[128,128]{1,0:T(8,128)S(1)} %cholesky.603), custom_call_target="Cholesky" | custom-call | tf_op jit(solution)/shard_map/jit(cholesky)/cholesky | solution.py:34
  249.7 10.2 %custom-call.38 = f32[1,128,128]{1,2,0:T(8,128)S(1)} custom-call(f32[1,128,128]{2,1,0:T(8,128)S(1)} %get-tuple-element.79), custom_call_target="InvertDiagBlocksLowerTriangular" | custom-call | tf_op jit(solution)/shard_map/jit(cholesky)/cholesky | solution.py:34
  261.5 11.7 %cholesky.486 = f32[128,128]{1,0:T(8,128)S(1)} custom-call(f32[128,128]{1,0:T(8,128)S(1)} %cholesky.608), custom_call_target="Cholesky" | custom-call | tf_op jit(solution)/shard_map/jit(cholesky)/cholesky | solution.py:34
  273.9 9.8 %custom-call.39 = f32[1,128,128]{1,2,0:T(8,128)S(1)} custom-call(f32[1,128,128]{2,1,0:T(8,128)S(1)} %get-tuple-element.76), custom_call_target="InvertDiagBlocksLowerTriangular" | custom-call | tf_op jit(solution)/shard_map/jit(cholesky)/cholesky | solution.py:34
  285.2 11.9 %cholesky.503 = f32[128,128]{1,0:T(8,128)S(1)} custom-call(f32[128,128]{1,0:T(8,128)S(1)} %convolution_subtract_fusion.25), custom_call_target="Cholesky" | custom-call | tf_op jit(solution)/shard_map/jit(cholesky)/cholesky | solution.py:34
  316.5 11.7 %cholesky.374 = f32[128,128]{1,0:T(8,128)S(1)} custom-call(f32[128,128]{1,0:T(8,128)S(1)} %cholesky.586), custom_call_target="Cholesky" | custom-call | tf_op jit(solution)/shard_map/jit(cholesky)/cholesky | solution.py:34
  328.2 9.8 %custom-call.33 = f32[1,128,128]{1,2,0:T(8,128)S(1)} custom-call(f32[1,128,128]{2,1,0:T(8,128)S(1)} %get-tuple-element.92), custom_call_target="InvertDiagBlocksLowerTriangular" | custom-call | tf_op jit(solution)/shard_map/jit(cholesky)/cholesky | solution.py:34
  340.7 11.7 %cholesky.393 = f32[128,128]{1,0:T(8,128)S(1)} custom-call(f32[128,128]{1,0:T(8,128)S(1)} %cholesky.590), custom_call_target="Cholesky" | custom-call | tf_op jit(solution)/shard_map/jit(cholesky)/cholesky | solution.py:34
  353.8 10.2 %custom-call.34 = f32[1,128,128]{1,2,0:T(8,128)S(1)} custom-call(f32[1,128,128]{2,1,0:T(8,128)S(1)} %get-tuple-element.89), custom_call_target="InvertDiagBlocksLowerTriangular" | custom-call | tf_op jit(solution)/shard_map/jit(cholesky)/cholesky | solution.py:34
  365.6 11.7 %cholesky.414 = f32[128,128]{1,0:T(8,128)S(1)} custom-call(f32[128,128]{1,0:T(8,128)S(1)} %cholesky.595), custom_call_target="Cholesky" | custom-call | tf_op jit(solution)/shard_map/jit(cholesky)/cholesky | solution.py:34
  378.0 9.8 %custom-call.35 = f32[1,128,128]{1,2,0:T(8,128)S(1)} custom-call(f32[1,128,128]{2,1,0:T(8,128)S(1)} %get-tuple-element.86), custom_call_target="InvertDiagBlocksLowerTriangular" | custom-call | tf_op jit(solution)/shard_map/jit(cholesky)/cholesky | solution.py:34
  389.3 11.9 %cholesky.431 = f32[128,128]{1,0:T(8,128)S(1)} custom-call(f32[128,128]{1,0:T(8,128)S(1)} %convolution_subtract_fusion.26), custom_call_target="Cholesky" | custom-call | tf_op jit(solution)/shard_map/jit(cholesky)/cholesky | solution.py:34
  405.5 11.9 %while.6 = (s32[]{:T(128)}, f32[512,512]{1,0:T(8,128)}, s32[4,2]{0,1:T(2,128)S(1)}, f32[4,128,128]{2,1,0:T(8,128)S(1)}, s32[]{:T(128)}) while((s32[]{:T(128)}, f32[512,512]{1,0:T(8,128)}, s32[4,2]{0,1:T(2,128)S(1)}, f32[4,128,128]{2,1,0:T(8,128)S(1)}, s32[]{:T(128)}) %tuple.99), condition=%wide.while_cond, body=%wide.while_body.sunk | while | flops 2 | bytes 131181 | solution.py:35
  417.4 11.5 %fusion.237 = f32[512,4096]{0,1:T(8,128)} fusion(bf16[512,1024]{1,0:T(8,128)(2,1)} %get-tuple-element.54, bf16[4096,1024]{1,0:T(8,128)(2,1)} %param.7), kind=kOutput, calls=%fused_computation.375 | convolution fusion | flops 4294967296 | bytes 17825792 | tf_op jit(solution)/shard_map/dot_general | solution.py:12
  428.9 39.3 %custom-call.36 = f32[4,128,128]{1,2,0:T(8,128)S(1)} custom-call(f32[4,128,128]{2,1,0:T(8,128)S(1)} %get-tuple-element.24), custom_call_target="InvertDiagBlocksLowerTriangular" | custom-call | tf_op jit(solution)/shard_map/jit(_cho_solve)/triangular_solve | solution.py:35
  485.5 12.8 %fusion.21 = f32[4096,256]{1,0:T(8,128)} fusion(f32[4096,256]{1,0:T(8,128)} %param.9, f32[512,4096]{0,1:T(8,128)} %fusion.237, f32[4096,256]{1,0:T(8,128)} %scatter_custom_fusion.1, f32[512]{0:T(512)S(1)} %multiply_reduce_fusion.3, f32[4096]{0:T(1024)S(1)} %multiply_reduce_fusion, f32[128,256]{1,0:T(8,128)S(1)} %fusion.197, f32[128,256]{1,0:T(8,128)S(1)} %fusion.195, ...), kind=kOutput, calls=%fused_computation.38 | convolution fusion | flops 6454378496 | bytes 21514240 | tf_op jit(solution)/shard_map/dot_general | solution.py:36
  504.7 11.5 %fusion.238 = f32[512,4096]{0,1:T(8,128)} fusion(bf16[512,1024]{1,0:T(8,128)(2,1)} %get-tuple-element.55, bf16[4096,1024]{1,0:T(8,128)(2,1)} %param.7), kind=kOutput, calls=%fused_computation.376 | convolution fusion | flops 4294967296 | bytes 17825792 | tf_op jit(solution)/shard_map/dot_general | solution.py:12
  516.2 40.5 %custom-call.40 = f32[4,128,128]{1,2,0:T(8,128)S(1)} custom-call(f32[4,128,128]{2,1,0:T(8,128)} %copy-done.3), custom_call_target="InvertDiagBlocksLowerTriangular" | custom-call | tf_op jit(solution)/shard_map/jit(_cho_solve)/triangular_solve | solution.py:35
  574.0 12.9 %fusion.27 = f32[4096,256]{1,0:T(8,128)} fusion(f32[4096,256]{1,0:T(8,128)} %fusion.21, f32[512,4096]{0,1:T(8,128)} %fusion.238, f32[4096,256]{1,0:T(8,128)} %scatter_custom_fusion.3, f32[512]{0:T(512)S(1)} %multiply_reduce_fusion.2, f32[4096]{0:T(1024)S(1)} %multiply_reduce_fusion, f32[128,256]{1,0:T(8,128)S(1)} %fusion.204, f32[128,256]{1,0:T(8,128)S(1)} %fusion.202, ...), kind=kOutput, calls=%fused_computation.40 | convolution fusion | flops 6454378496 | bytes 21514240 | tf_op jit(solution)/shard_map/dot_general | solution.py:36
  591.7 11.5 %fusion.239 = f32[512,4096]{0,1:T(8,128)} fusion(bf16[512,1024]{1,0:T(8,128)(2,1)} %get-tuple-element.56, bf16[4096,1024]{1,0:T(8,128)(2,1)} %param.7), kind=kOutput, calls=%fused_computation.377 | convolution fusion | flops 4294967296 | bytes 17825792 | tf_op jit(solution)/shard_map/dot_general | solution.py:12
  603.2 40.1 %custom-call.44 = f32[4,128,128]{1,2,0:T(8,128)S(1)} custom-call(f32[4,128,128]{2,1,0:T(8,128)} %copy-done.2), custom_call_target="InvertDiagBlocksLowerTriangular" | custom-call | tf_op jit(solution)/shard_map/jit(_cho_solve)/triangular_solve | solution.py:35
  673.5 13.0 %fusion.33 = f32[4096,256]{1,0:T(8,128)} fusion(f32[4096,256]{1,0:T(8,128)} %fusion.27, f32[512,4096]{0,1:T(8,128)} %fusion.239, f32[4096,256]{1,0:T(8,128)} %scatter_custom_fusion.5, f32[512]{0:T(512)S(1)} %multiply_reduce_fusion.1, f32[4096]{0:T(1024)S(1)} %multiply_reduce_fusion, f32[128,256]{1,0:T(8,128)S(1)} %fusion.211, f32[128,256]{1,0:T(8,128)S(1)} %fusion.209, ...), kind=kOutput, calls=%fused_computation.42 | convolution fusion | flops 6454378496 | bytes 21514240 | tf_op jit(solution)/shard_map/dot_general | solution.py:36
  (199 shorter events, 209.3 us)
Async XLA Ops:
  7.2 4.5 copy-start.4
  7.2 101.5 %all-reduce.13.cloned.1.call-start = ((), (), s32[]{:S(2)}) async-start(), calls=%async_computation.3 | async-start | bytes 6291456 | tf_op jit(solution)/shard_map/psum | solution.py:29
  36.4 431.9 %all-reduce.7.cloned.1.call-start = ((), (), s32[]{:S(2)}) async-start(), calls=%async_computation | async-start | bytes 1048576 | tf_op jit(solution)/shard_map/psum | solution.py:30
  41.1 518.7 %all-reduce.9.cloned.1.call-start = ((), (), s32[]{:S(2)}) async-start(), calls=%async_computation.1 | async-start | bytes 1048576 | tf_op jit(solution)/shard_map/psum | solution.py:30
  206.1 0.7 copy-start.2
  211.4 1.0 copy-start
  308.8 6.7 copy-start.3
  315.5 1.0 copy-start.1
  504.7 154.8 %all-reduce.11.cloned.1.call-start = ((), (), s32[]{:S(2)}) async-start(), calls=%async_computation.2 | async-start | bytes 1048576 | tf_op jit(solution)/shard_map/psum | solution.py:30
Sparse Core Ops, SparseCore 0:
  36.5 72.1 all-reduce.12
  111.8 55.1 all-reduce.6
  504.8 55.0 all-reduce.8
  591.8 54.6 all-reduce.10
where the time goes:
time: 710 us; the launch traced here: 701 us
  other arithmetic  421 us (59%)
  matrix products  120 us (17%)
  local copies, waits for them, and re-layouts  71.3 us (10%)
  waiting for transfers between devices  65.4 us (9%)
  between operations  22.8 us (3%)
    another operation x45, other arithmetic, local(): jnp.linalg.cholesky(block_kernel + RIDGE * jnp.eye(block_size, dtype=jnp....  239 us
    another operation x7, other arithmetic, local(): update = jax.scipy.linalg.cho_solve((factor, True), block_res)  121 us
    psum x1, waiting for transfers between devices, local(): summed = lax.psum(owned_rows.astype(jnp.bfloat16), 'pts')  62.1 us
    dot_general x6, matrix products, kernel(): lax.dot_general(left_rows, right_rows, (((1,), (1,)), ((), ())), preferre...  42 us
    dot_general x3, matrix products, local(): product = jnp.dot(kernel_rows, update, precision=lax.Precision.HIGHEST)  38.7 us
    another operation x40, local copies, waits for them, and re-layouts, local(): update = jax.scipy.linalg.cho_solve((factor, True), block_res)  28.3 us
    another operation x42, matrix products, local(): update = jax.scipy.linalg.cho_solve((factor, True), block_res)  26.9 us
    scatter-add x3, other arithmetic, local(): coefficients = coefficients.at[clipped].add(own_update)  24 us
  transfers between devices with their start and end apart: 4, of which 2 were waited for; matrix products, arithmetic and copies ran while one was open for 68% of the time, Pallas kernels for 0%

commit v1 on v0

--- a/solution.py
+++ b/solution.py
@@ -1,9 +1,17 @@
+import functools
 import jax
 import jax.numpy as jnp
 from jax import lax
 from jax.sharding import PartitionSpec as P
 
 RIDGE = 0.5
+
+
+def close_the_indices(state, net_axis):
+    return jnp.sum(lax.all_gather(state, net_axis), axis=0)
+
+
+words_step_on = functools.partial(close_the_indices, net_axis="pts")
 
 
 def kernel(left_rows, right_rows, inverse_width):
@@ -26,7 +34,7 @@
         clipped = jnp.clip(offsets, 0, local_count - 1)
         owned_rows = jnp.where(is_owned[:, None], points[clipped].astype(jnp.float32), 0.0)
         owned_res = jnp.where(is_owned[:, None], residual[clipped], 0.0)
-        summed = lax.psum(owned_rows.astype(jnp.bfloat16), "pts")
+        summed = words_step_on(owned_rows.astype(jnp.bfloat16))
         block_res = lax.psum(owned_res, "pts")
         kernel_rows = kernel(points, summed, inverse_width)
         block_kernel = kernel(summed, summed, inverse_width)

time: 710 us -> 832 us (1.17)
  waiting for transfers between devices: 65.4 us -> 158 us
  matrix products: 120 us -> 136 us
  other arithmetic: 421 us -> 434 us
    all_gather x0 -> x3, waiting for transfers between devices: none -> 108 us  [close_the_indices(): return jnp.sum(lax.all_gather(state, net_axis), axis=0)]
    psum x1 -> x0, waiting for transfers between devices: 62.1 us -> none  [local(): summed = lax.psum(owned_rows.astype(jnp.bfloat16), 'pts')]
    psum x3, waiting for transfers between devices: 3.15 us -> 50.2 us  [local(): block_res = lax.psum(owned_res, 'pts')]
    dot_general x3, matrix products: 38.7 us -> 57.2 us  [local(): product = jnp.dot(kernel_rows, update, precision=lax.Precision.HIGHEST)]
    reduce_sum x0 -> x3, other arithmetic: none -> 17 us  [close_the_indices(): return jnp.sum(lax.all_gather(state, net_axis), axis=0)]
    another operation x45 -> x42, other arithmetic: 239 us -> 239 us  [local(): jnp.linalg.cholesky(block_kernel + RIDGE * jnp.eye(block_size, dtype=jnp....]
  transfers between devices with their start and end apart: 4 -> 6, of which waited for: 2 -> 4; matrix products, arithmetic and copies ran while one was open for 68% -> 61% of each run, Pallas kernels for 0% -> 0%
where the time goes in v1:
time: 832 us; the launch traced here: 824 us
  other arithmetic  434 us (52%)
  waiting for transfers between devices  158 us (19%)
  matrix products  136 us (16%)
  local copies, waits for them, and re-layouts  71.5 us (9%)
  between operations  22.7 us (3%)
    another operation x42, other arithmetic, local(): jnp.linalg.cholesky(block_kernel + RIDGE * jnp.eye(block_size, dtype=jnp....  239 us
    another operation x7, other arithmetic, local(): update = jax.scipy.linalg.cho_solve((factor, True), block_res)  121 us
    all_gather x3, waiting for transfers between devices, close_the_indices(): return jnp.sum(lax.all_gather(state, net_axis), axis=0)  108 us
    dot_general x3, matrix products, local(): product = jnp.dot(kernel_rows, update, precision=lax.Precision.HIGHEST)  57.2 us
    psum x3, waiting for transfers between devices, local(): block_res = lax.psum(owned_res, 'pts')  50.2 us
    dot_general x6, matrix products, kernel(): lax.dot_general(left_rows, right_rows, (((1,), (1,)), ((), ())), preferre...  35.6 us
    another operation x40, local copies, waits for them, and re-layouts, local(): update = jax.scipy.linalg.cho_solve((factor, True), block_res)  27.8 us
    another operation x42, matrix products, local(): update = jax.scipy.linalg.cho_solve((factor, True), block_res)  26.9 us
  transfers between devices with their start and end apart: 6, of which 4 were waited for; matrix products, arithmetic and copies ran while one was open for 61% of the time, Pallas kernels for 0%

profile of v1, /device:TPU:0, one launch (start us, length us, event | category | flops | bytes accessed | tf_op | source)
XLA Modules:
  0.0 823.8 jit_solution(9572671621633139903)
XLA Ops:
  48.6 28.8 %all-gather.4.cloned.1.call-done = bf16[8,512,1024]{2,1,0:T(8,128)(2,1)} async-done(((bf16[1,512,1024]{2,1,0:T(8,128)(2,1)}), bf16[8,512,1024]{2,1,0:T(8,128)(2,1)}) %all-gather.4.cloned.1.call-update) | async-done | bytes 8388624 | tf_op jit(solution)/shard_map/all_gather | solution.py:11
  83.3 10.6 %fusion.240 = f32[512,4096]{1,0:T(8,128)} fusion(bf16[512,1024]{1,0:T(8,128)(2,1)S(1)} %reduce_sum.77, bf16[4096,1024]{1,0:T(8,128)(2,1)} %param.7), kind=kOutput, calls=%fused_computation.378 | convolution fusion | flops 4294967296 | bytes 17825792 | tf_op jit(solution)/shard_map/dot_general | solution.py:20
  93.9 39.6 %all-gather.6.cloned.1.call-done = bf16[8,512,1024]{2,1,0:T(8,128)(2,1)} async-done(((bf16[1,512,1024]{2,1,0:T(8,128)(2,1)}), bf16[8,512,1024]{2,1,0:T(8,128)(2,1)}) %all-gather.6.cloned.1.call-update) | async-done | bytes 8388624 | tf_op jit(solution)/shard_map/all_gather | solution.py:11
  139.5 10.5 %fusion.241 = f32[512,4096]{1,0:T(8,128)} fusion(bf16[512,1024]{1,0:T(8,128)(2,1)S(1)} %reduce_sum.79, bf16[4096,1024]{1,0:T(8,128)(2,1)} %param.7), kind=kOutput, calls=%fused_computation.379 | convolution fusion | flops 4294967296 | bytes 17825792 | tf_op jit(solution)/shard_map/dot_general | solution.py:20
  150.0 39.7 %all-gather.8.cloned.1.call-done = bf16[8,512,1024]{2,1,0:T(8,128)(2,1)} async-done(((bf16[1,512,1024]{2,1,0:T(8,128)(2,1)}), bf16[8,512,1024]{2,1,0:T(8,128)(2,1)}) %all-gather.8.cloned.1.call-update) | async-done | bytes 8388624 | tf_op jit(solution)/shard_map/all_gather | solution.py:11
  195.7 10.4 %fusion.242 = f32[512,4096]{1,0:T(8,128)} fusion(bf16[512,1024]{1,0:T(8,128)(2,1)S(1)} %reduce_sum.85, bf16[4096,1024]{1,0:T(8,128)(2,1)} %param.7), kind=kOutput, calls=%fused_computation.380 | convolution fusion | flops 4294967296 | bytes 17825792 | tf_op jit(solution)/shard_map/dot_general | solution.py:20
  208.5 11.7 %cholesky.518 = f32[128,128]{1,0:T(8,128)S(1)} custom-call(f32[128,128]{1,0:T(8,128)S(1)} %cholesky.612), custom_call_target="Cholesky" | custom-call | tf_op jit(solution)/shard_map/jit(cholesky)/cholesky | solution.py:42
  220.3 9.8 %custom-call.41 = f32[1,128,128]{1,2,0:T(8,128)S(1)} custom-call(f32[1,128,128]{2,1,0:T(8,128)S(1)} %get-tuple-element.69), custom_call_target="InvertDiagBlocksLowerTriangular" | custom-call | tf_op jit(solution)/shard_map/jit(cholesky)/cholesky | solution.py:42
  232.7 11.7 %cholesky.537 = f32[128,128]{1,0:T(8,128)S(1)} custom-call(f32[128,128]{1,0:T(8,128)S(1)} %cholesky.616), custom_call_target="Cholesky" | custom-call | tf_op jit(solution)/shard_map/jit(cholesky)/cholesky | solution.py:42
  244.5 10.0 %custom-call.42 = f32[1,128,128]{1,2,0:T(8,128)S(1)} custom-call(f32[1,128,128]{2,1,0:T(8,128)S(1)} %get-tuple-element.66), custom_call_target="InvertDiagBlocksLowerTriangular" | custom-call | tf_op jit(solution)/shard_map/jit(cholesky)/cholesky | solution.py:42
  256.1 11.7 %cholesky.558 = f32[128,128]{1,0:T(8,128)S(1)} custom-call(f32[128,128]{1,0:T(8,128)S(1)} %cholesky.621), custom_call_target="Cholesky" | custom-call | tf_op jit(solution)/shard_map/jit(cholesky)/cholesky | solution.py:42
  279.6 12.7 %cholesky.575 = f32[128,128]{1,0:T(8,128)} custom-call(f32[128,128]{1,0:T(8,128)S(1)} %convolution_subtract_fusion.24), custom_call_target="Cholesky" | custom-call | tf_op jit(solution)/shard_map/jit(cholesky)/cholesky | solution.py:42
  294.8 11.7 %cholesky.446 = f32[128,128]{1,0:T(8,128)S(1)} custom-call(f32[128,128]{1,0:T(8,128)S(1)} %cholesky.599), custom_call_target="Cholesky" | custom-call | tf_op jit(solution)/shard_map/jit(cholesky)/cholesky | solution.py:42
  306.5 9.8 %custom-call.37 = f32[1,128,128]{1,2,0:T(8,128)S(1)} custom-call(f32[1,128,128]{2,1,0:T(8,128)S(1)} %get-tuple-element.79), custom_call_target="InvertDiagBlocksLowerTriangular" | custom-call | tf_op jit(solution)/shard_map/jit(cholesky)/cholesky | solution.py:42
  319.0 11.7 %cholesky.465 = f32[128,128]{1,0:T(8,128)S(1)} custom-call(f32[128,128]{1,0:T(8,128)S(1)} %cholesky.603), custom_call_target="Cholesky" | custom-call | tf_op jit(solution)/shard_map/jit(cholesky)/cholesky | solution.py:42
  330.9 9.8 %custom-call.38 = f32[1,128,128]{1,2,0:T(8,128)S(1)} custom-call(f32[1,128,128]{2,1,0:T(8,128)S(1)} %get-tuple-element.76), custom_call_target="InvertDiagBlocksLowerTriangular" | custom-call | tf_op jit(solution)/shard_map/jit(cholesky)/cholesky | solution.py:42
  342.3 11.7 %cholesky.486 = f32[128,128]{1,0:T(8,128)S(1)} custom-call(f32[128,128]{1,0:T(8,128)S(1)} %cholesky.608), custom_call_target="Cholesky" | custom-call | tf_op jit(solution)/shard_map/jit(cholesky)/cholesky | solution.py:42
  366.0 12.1 %cholesky.503 = f32[128,128]{1,0:T(8,128)S(1)} custom-call(f32[128,128]{1,0:T(8,128)S(1)} %convolution_subtract_fusion.25), custom_call_target="Cholesky" | custom-call | tf_op jit(solution)/shard_map/jit(cholesky)/cholesky | solution.py:42
  396.9 11.7 %cholesky.374 = f32[128,128]{1,0:T(8,128)S(1)} custom-call(f32[128,128]{1,0:T(8,128)S(1)} %cholesky.586), custom_call_target="Cholesky" | custom-call | tf_op jit(solution)/shard_map/jit(cholesky)/cholesky | solution.py:42
  408.6 9.8 %custom-call.33 = f32[1,128,128]{1,2,0:T(8,128)S(1)} custom-call(f32[1,128,128]{2,1,0:T(8,128)S(1)} %get-tuple-element.89), custom_call_target="InvertDiagBlocksLowerTriangular" | custom-call | tf_op jit(solution)/shard_map/jit(cholesky)/cholesky | solution.py:42
  421.1 11.7 %cholesky.393 = f32[128,128]{1,0:T(8,128)S(1)} custom-call(f32[128,128]{1,0:T(8,128)S(1)} %cholesky.590), custom_call_target="Cholesky" | custom-call | tf_op jit(solution)/shard_map/jit(cholesky)/cholesky | solution.py:42
  432.8 9.9 %custom-call.34 = f32[1,128,128]{1,2,0:T(8,128)S(1)} custom-call(f32[1,128,128]{2,1,0:T(8,128)S(1)} %get-tuple-element.86), custom_call_target="InvertDiagBlocksLowerTriangular" | custom-call | tf_op jit(solution)/shard_map/jit(cholesky)/cholesky | solution.py:42
  444.4 11.7 %cholesky.414 = f32[128,128]{1,0:T(8,128)S(1)} custom-call(f32[128,128]{1,0:T(8,128)S(1)} %cholesky.595), custom_call_target="Cholesky" | custom-call | tf_op jit(solution)/shard_map/jit(cholesky)/cholesky | solution.py:42
  468.0 11.9 %cholesky.431 = f32[128,128]{1,0:T(8,128)S(1)} custom-call(f32[128,128]{1,0:T(8,128)S(1)} %convolution_subtract_fusion.26), custom_call_target="Cholesky" | custom-call | tf_op jit(solution)/shard_map/jit(cholesky)/cholesky | solution.py:42
  484.8 11.3 %while.6 = (s32[]{:T(128)}, f32[512,512]{1,0:T(8,128)}, s32[4,2]{0,1:T(2,128)S(1)}, f32[4,128,128]{2,1,0:T(8,128)S(1)}, s32[]{:T(128)}) while((s32[]{:T(128)}, f32[512,512]{1,0:T(8,128)}, s32[4,2]{0,1:T(2,128)S(1)}, f32[4,128,128]{2,1,0:T(8,128)S(1)}, s32[]{:T(128)}) %tuple.104), condition=%wide.while_cond, body=%wide.while_body.sunk | while | flops 2 | bytes 131181 | solution.py:43
  496.1 40.1 %custom-call.40 = f32[4,128,128]{1,2,0:T(8,128)S(1)} custom-call(f32[4,128,128]{2,1,0:T(8,128)} %copy-done.5), custom_call_target="InvertDiagBlocksLowerTriangular" | custom-call | tf_op jit(solution)/shard_map/jit(_cho_solve)/triangular_solve | solution.py:43
  536.2 39.3 %custom-call.36 = f32[4,128,128]{1,2,0:T(8,128)S(1)} custom-call(f32[4,128,128]{2,1,0:T(8,128)S(1)} %get-tuple-element.24), custom_call_target="InvertDiagBlocksLowerTriangular" | custom-call | tf_op jit(solution)/shard_map/jit(_cho_solve)/triangular_solve | solution.py:43
  594.9 19.0 %fusion.21 = f32[4096,256]{1,0:T(8,128)} fusion(f32[4096,256]{1,0:T(8,128)} %param.9, f32[512,4096]{1,0:T(8,128)} %fusion.240, f32[4096,256]{1,0:T(8,128)} %scatter_custom_fusion.1, f32[512]{0:T(512)S(1)} %multiply_reduce_fusion.3, f32[4096]{0:T(1024)S(1)} %multiply_reduce_fusion, f32[128,256]{1,0:T(8,128)S(1)} %fusion.200, f32[128,256]{1,0:T(8,128)S(1)} %fusion.198, ...), kind=kOutput, calls=%fused_computation.38 | convolution fusion | flops 6454378496 | bytes 21514240 | tf_op jit(solution)/shard_map/dot_general | solution.py:44
  623.2 50.2 %all-reduce.7.cloned.1.call-done = f32[512,256]{1,0:T(8,128)} async-done(((f32[512,256]{1,0:T(8,128)}), f32[512,256]{1,0:T(8,128)}) %all-reduce.7.cloned.1.call-update) | async-done | bytes 524304 | tf_op jit(solution)/shard_map/psum | solution.py:38
  687.7 19.0 %fusion.27 = f32[4096,256]{1,0:T(8,128)} fusion(f32[4096,256]{1,0:T(8,128)} %fusion.21, f32[512,4096]{1,0:T(8,128)} %fusion.241, f32[4096,256]{1,0:T(8,128)} %scatter_custom_fusion.3, f32[512]{0:T(512)S(1)} %multiply_reduce_fusion.2, f32[4096]{0:T(1024)S(1)} %multiply_reduce_fusion, f32[128,256]{1,0:T(8,128)S(1)} %fusion.207, f32[128,256]{1,0:T(8,128)S(1)} %fusion.205, ...), kind=kOutput, calls=%fused_computation.40 | convolution fusion | flops 6454378496 | bytes 21514240 | tf_op jit(solution)/shard_map/dot_general | solution.py:44
  720.0 39.3 %custom-call.44 = f32[4,128,128]{1,2,0:T(8,128)S(1)} custom-call(f32[4,128,128]{2,1,0:T(8,128)S(1)} %get-tuple-element.26), custom_call_target="InvertDiagBlocksLowerTriangular" | custom-call | tf_op jit(solution)/shard_map/jit(_cho_solve)/triangular_solve | solution.py:43
  789.7 19.2 %fusion.33 = f32[4096,256]{1,0:T(8,128)} fusion(f32[4096,256]{1,0:T(8,128)} %fusion.27, f32[512,4096]{1,0:T(8,128)} %fusion.242, f32[4096,256]{1,0:T(8,128)} %scatter_custom_fusion.5, f32[512]{0:T(512)S(1)} %multiply_reduce_fusion.1, f32[4096]{0:T(1024)S(1)} %multiply_reduce_fusion, f32[128,256]{1,0:T(8,128)S(1)} %fusion.214, f32[128,256]{1,0:T(8,128)S(1)} %fusion.212, ...), kind=kOutput, calls=%fused_computation.42 | convolution fusion | flops 6454378496 | bytes 21514240 | tf_op jit(solution)/shard_map/dot_general | solution.py:44
  (212 shorter events, 250.6 us)
Async XLA Ops:
  7.2 4.5 copy-start.7
  7.2 70.2 %all-gather.4.cloned.1.call-start = ((), (), s32[]{:S(2)}) async-start(), calls=%async_computation | async-start | bytes 9437184 | tf_op jit(solution)/shard_map/all_gather | solution.py:11
  20.2 113.3 %all-gather.6.cloned.1.call-start = ((), (), s32[]{:S(2)}) async-start(), calls=%async_computation.2 | async-start | bytes 9437184 | tf_op jit(solution)/shard_map/all_gather | solution.py:11
  28.7 161.0 %all-gather.8.cloned.1.call-start = ((), (), s32[]{:S(2)}) async-start(), calls=%async_computation.4 | async-start | bytes 9437184 | tf_op jit(solution)/shard_map/all_gather | solution.py:11
  38.2 539.4 %all-reduce.5.cloned.1.call-start = ((), (), s32[]{:S(2)}) async-start(), calls=%async_computation.1 | async-start | bytes 1048576 | tf_op jit(solution)/shard_map/psum | solution.py:38
  43.0 630.5 %all-reduce.7.cloned.1.call-start = ((), (), s32[]{:S(2)}) async-start(), calls=%async_computation.3 | async-start | bytes 1048576 | tf_op jit(solution)/shard_map/psum | solution.py:38
  83.0 10.9 %copy-start.1 = (bf16[512,1024]{1,0:T(8,128)(2,1)}, bf16[512,1024]{1,0:T(8,128)(2,1)S(1)}, u32[]{:S(2)}) copy-start(bf16[512,1024]{1,0:T(8,128)(2,1)S(1)} %reduce_sum.77) | copy-start | bytes 3145732
  207.4 1.1 copy-start.4
  293.7 1.1 copy-start.2
  390.6 5.2 copy-start.5
  395.9 1.0 copy-start.3
  442.8 53.3 %copy-start.6 = (f32[128,128]{1,0:T(8,128)S(1)}, f32[128,128]{1,0:T(8,128)}, u32[]{:S(2)}) copy-start(f32[128,128]{1,0:T(8,128)} %cholesky.575) | copy-start | bytes 196612
  618.7 156.9 %all-reduce.9.cloned.1.call-start = ((), (), s32[]{:S(2)}) async-start(), calls=%async_computation.5 | async-start | bytes 1048576 | tf_op jit(solution)/shard_map/psum | solution.py:38
  706.7 4.9 copy-start
Sparse Core Ops, SparseCore 0:
  20.3 56.9 all-gather.3
  79.2 54.2 all-gather.5
  135.4 54.2 all-gather.7
  192.7 55.3 all-reduce.4
  618.8 54.6 all-reduce.6
  711.7 54.4 all-reduce.8
